TPU v7x, 32 devices: a whole 2x2x4 slice. The times are simulated.
32 devices in a mesh: dp: 8 (over z, core), chan: 4 (over y, x).
Axes of the slice: x: 2, y: 2, z: 4, core: 2. Of those that a mesh axis runs over, the one named last changes fastest.
Arguments:
- images: bfloat16 [16, 16, 16, 2816], P('dp', None, None, 'chan'), may hold values from -6 to 6
- kernel: float32 [7, 7, 2816], P(None, None, 'chan'), may hold values from -0.875 to 0.875
- layernorm_gain: float32 [2816], P('chan'), may hold values from 0.25 to 1.75
- layernorm_bias: float32 [2816], P('chan'), may hold values from -3 to 3
- w_expand: bfloat16 [2816, 11264], P('dp', 'chan'), may hold values from -0.109375 to 0.109375
- w_reduce: bfloat16 [11264, 2816], P('chan', 'dp'), may hold values from -0.0546875 to 0.0546875
- layer_scale: float32 [2816], P('chan'), may hold values from 0.25 to 1
- cotangent: bfloat16 [16, 16, 16, 2816], P('dp', None, None, 'chan'), may hold values from -6 to 6
Outputs:
- output: bfloat16 [16, 16, 16, 2816], P('dp', None, None, 'chan')
- grad_images: bfloat16 [16, 16, 16, 2816], P('dp', None, None, 'chan')
- grad_kernel: float32 [7, 7, 2816], P(None, None, 'chan')
- gain_gradient: float32 [2816], P('chan')
- grad_bias: float32 [2816], P('chan')
- grad_expand: float32 [2816, 11264], P('dp', 'chan')
- grad_reduce: float32 [11264, 2816], P('chan', 'dp')
- grad_scale: float32 [2816], P('chan')
All inputs are finite; a program needn't handle non-finite values.
Results may differ from a plain program's by a relative error of at most 0.025.
Values may be sent and summed in bfloat16 or wider, within the bound.
A program may use at most 128 MiB of HBM per device.

v0:
```python
import math
import jax
import jax.numpy as jnp
from jax import lax
from jax.sharding import PartitionSpec as P

eps = 1e-06


def depthwise(field, kern):
    height = field.shape[1]
    breadth = field.shape[2]
    padded = jnp.pad(field, ((0, 0), (3, 3), (3, 3), (0, 0)))
    total = jnp.zeros(field.shape, jnp.float32)
    for i in range(7):
        for j in range(7):
            total = total + padded[:, i : i + height, j : j + breadth, :] * kern[i, j]
    return total


def normal_cdf(value):
    return 0.5 * (1.0 + jax.scipy.special.erf(value / math.sqrt(2.0)))


def body(
    images, kernel, layernorm_gain, layernorm_bias, w_expand, w_reduce, layer_scale, cotangent
):
    shape_in = images.shape
    height = shape_in[1]
    breadth = shape_in[2]
    positions = shape_in[0] * height * breadth
    local_chan = shape_in[3]
    image_width = local_chan * lax.axis_size("chan")
    xf = images.astype(jnp.float32)
    conv = depthwise(xf, kernel).reshape(positions, local_chan)
    mean_val = lax.psum(jnp.sum(conv, axis=1), "chan")[:, None] / image_width
    centred_rows = conv - mean_val
    var = lax.psum(jnp.sum(centred_rows * centred_rows, axis=1), "chan")[:, None] / image_width
    inverse_deviation = lax.rsqrt(var + eps)
    standardized_input = centred_rows * inverse_deviation
    normed_output = (standardized_input * layernorm_gain + layernorm_bias).astype(jnp.bfloat16)
    normed_all = lax.all_gather(normed_output, "chan", axis=1, tiled=True)
    expand_all = lax.all_gather(w_expand, "dp", axis=0, tiled=True)
    pre = jnp.dot(normed_all, expand_all, preferred_element_type=jnp.float32)
    hidden = (pre * normal_cdf(pre)).astype(jnp.bfloat16)
    reduce_all = lax.all_gather(w_reduce, "dp", axis=1, tiled=True)
    partial_branch = jnp.dot(hidden, reduce_all, preferred_element_type=jnp.float32)
    branch = lax.psum_scatter(
        partial_branch.astype(jnp.bfloat16), "chan", scatter_dimension=1, tiled=True
    ).astype(jnp.float32)
    xr = xf.reshape(positions, local_chan)
    output = (xr + layer_scale * branch).astype(jnp.bfloat16).reshape(shape_in)
    dyf = cotangent.astype(jnp.float32).reshape(positions, local_chan)
    scale_part = jnp.sum(dyf * branch, axis=0)
    dbranch = (dyf * layer_scale).astype(jnp.bfloat16)
    dbranch_all = lax.all_gather(dbranch, "chan", axis=1, tiled=True)
    dhidden = lax.dot_general(
        dbranch_all, reduce_all, (((1,), (1,)), ((), ())), preferred_element_type=jnp.float32
    )
    slope = normal_cdf(pre) + pre * jnp.exp(-0.5 * pre * pre) / math.sqrt(2.0 * math.pi)
    dpre = (dhidden * slope).astype(jnp.bfloat16)
    columns = normed_all
    grad_expand = lax.psum_scatter(
        lax.dot_general(
            columns, dpre, (((0,), (0,)), ((), ())), preferred_element_type=jnp.float32
        ).astype(jnp.bfloat16),
        "dp",
        scatter_dimension=0,
        tiled=True,
    ).astype(jnp.float32)
    partial_normed = lax.dot_general(
        dpre, expand_all, (((1,), (1,)), ((), ())), preferred_element_type=jnp.float32
    )
    normed_grad = lax.psum_scatter(
        partial_normed.astype(jnp.bfloat16), "chan", scatter_dimension=1, tiled=True
    ).astype(jnp.float32)
    columns = dbranch_all
    grad_reduce = (
        lax.psum_scatter(
            lax.dot_general(
                columns, hidden, (((0,), (0,)), ((), ())), preferred_element_type=jnp.float32
            ).astype(jnp.bfloat16),
            "dp",
            scatter_dimension=0,
            tiled=True,
        )
        .astype(jnp.float32)
        .T
    )
    gain_partial = jnp.sum(normed_grad * standardized_input, axis=0)
    bias_part = jnp.sum(normed_grad, axis=0)
    standardized_grad = normed_grad * layernorm_gain
    first_half, second_half = lax.psum(
        (
            jnp.sum(standardized_grad, axis=1),
            jnp.sum(standardized_grad * standardized_input, axis=1),
        ),
        "chan",
    )
    conv_output_grad = inverse_deviation * (
        standardized_grad
        - first_half[:, None] / image_width
        - standardized_input * (second_half[:, None] / image_width)
    )
    conv_output_grad = conv_output_grad.reshape(shape_in)
    padded = jnp.pad(xf, ((0, 0), (3, 3), (3, 3), (0, 0)))
    dpad = jnp.pad(conv_output_grad, ((0, 0), (3, 3), (3, 3), (0, 0)))
    back = cotangent.astype(jnp.float32)
    kern_rows = []
    for i in range(7):
        tap_row = []
        for j in range(7):
            tap_row.append(
                jnp.sum(
                    padded[:, i : i + height, j : j + breadth, :] * conv_output_grad, axis=(0, 1, 2)
                )
            )
            back = back + dpad[:, 6 - i : 6 - i + height, 6 - j : 6 - j + breadth, :] * kernel[i, j]
        kern_rows.append(jnp.stack(tap_row))
    kernel_part = jnp.stack(kern_rows)
    grad_images = back.astype(jnp.bfloat16)
    grad_kernel, gain_gradient, grad_bias, grad_scale = (
        lax.psum(kernel_part.astype(jnp.bfloat16), "dp").astype(jnp.float32),
        lax.psum(gain_partial.astype(jnp.bfloat16), "dp").astype(jnp.float32),
        lax.psum(bias_part.astype(jnp.bfloat16), "dp").astype(jnp.float32),
        lax.psum(scale_part.astype(jnp.bfloat16), "dp").astype(jnp.float32),
    )
    return (
        output,
        grad_images,
        grad_kernel,
        gain_gradient,
        grad_bias,
        grad_expand,
        grad_reduce,
        grad_scale,
    )


def solution(mesh):
    in_specs = (
        P("dp", None, None, "chan"),
        P(None, None, "chan"),
        P("chan"),
        P("chan"),
        P("dp", "chan"),
        P("chan", "dp"),
        P("chan"),
        P("dp", None, None, "chan"),
    )
    out_specs = (
        P("dp", None, None, "chan"),
        P("dp", None, None, "chan"),
        P(None, None, "chan"),
        P("chan"),
        P("chan"),
        P("dp", "chan"),
        P("chan", "dp"),
        P("chan"),
    )
    return jax.shard_map(body, mesh=mesh, in_specs=in_specs, out_specs=out_specs, check_vma=False)
```

profile of v0, /device:TPU:0, one launch (start us, length us, event | category | flops | bytes accessed | tf_op | source)
XLA Modules:
  0.0 969.2 jit_solution(17701858807250672959)
XLA Ops:
  7.2 1.2 slice_reduce_fusion.46
  8.4 1.4 slice_reduce_fusion.48
  9.7 1.4 slice_reduce_fusion.47
  11.2 1.3 convert_element_type.71
  12.5 12.3 %fusion.114 = (f32[2,16,16]{2,1,0:T(8,128)S(1)}, f32[2,16,16,704]{3,2,1,0:T(8,128)S(1)}) fusion(f32[704]{0:T(1024)S(1)} %get-tuple-element.115, f32[704]{0:T(1024)S(1)} %get-tuple-element.116, f32[704]{0:T(1024)S(1)} %get-tuple-element.69, f32[704]{0:T(1024)S(1)} %get-tuple-element.70, f32[704]{0:T(1024)S(1)} %get-tuple-element.71, ...), kind=kLoop, calls=%fused_computation.336 | loop fusion | flops 35323392 | bytes 3023616 | tf_op jit(solution)/shard_map/reduce_sum | solution.py:36
  24.9 11.3 %psum.56 = f32[512]{0:T(512)S(1)} all-reduce(f32[512]{0:T(512)S(1)} %reduce_sum.512), channel_id=1, replica_groups=mesh['dp'=8,'chan'=4] {'chan'}, use_global_device_ids=true, to_apply=%region_1.2 | all-reduce | flops 512 | bytes 4096 | tf_op jit(solution)/shard_map/psum | solution.py:36
  36.7 8.0 psum.57
  44.7 1.9 copy.71
  46.6 1.1 add_convert_fusion
  47.8 0.7 all-gather.7.cloned.1.call-update
  48.5 0.7 all-gather.9.cloned.1.call-update
  49.2 0.3 reduce-scatter.5.cloned.1.call-start
  49.6 40.4 %all-gather.5.cloned.1.call-done = bf16[512,2816]{0,1:T(8,128)(2,1)} async-done(((bf16[512,704]{0,1:T(8,128)(2,1)}), bf16[512,2816]{0,1:T(8,128)(2,1)}) %all-gather.5.cloned.1.call-update) | async-done | bytes 2883600 | tf_op jit(solution)/shard_map/all_gather | solution.py:42
  90.0 145.3 %all-gather.7.cloned.1.call-done = bf16[2816,2816]{1,0:T(8,128)(2,1)} async-done(((bf16[352,2816]{1,0:T(8,128)(2,1)}), bf16[2816,2816]{1,0:T(8,128)(2,1)}) %all-gather.7.cloned.1.call-update) | async-done | bytes 15859728 | tf_op jit(solution)/shard_map/all_gather | solution.py:43
  235.3 15.1 %fusion.115 = f32[512,2816]{1,0:T(8,128)} fusion(bf16[512,2816]{0,1:T(8,128)(2,1)} %all-gather.5.cloned.1.call-done, bf16[2816,2816]{1,0:T(8,128)(2,1)} %all-gather.7.cloned.1.call-done), kind=kOutput, calls=%fused_computation.337 | convolution fusion | flops 8120172544 | bytes 24510464 | tf_op jit(solution)/shard_map/dot_general | solution.py:44
  250.3 128.5 %all-gather.9.cloned.1.call-done = bf16[2816,2816]{0,1:T(8,128)(2,1)} async-done(((bf16[2816,352]{0,1:T(8,128)(2,1)}), bf16[2816,2816]{0,1:T(8,128)(2,1)}) %all-gather.9.cloned.1.call-update) | async-done | bytes 15859728 | tf_op jit(solution)/shard_map/all_gather | solution.py:46
  378.8 16.3 %convolution_convert_fusion.3 = bf16[512,2816]{0,1:T(8,128)(2,1)} fusion(bf16[2816,2816]{0,1:T(8,128)(2,1)} %all-gather.9.cloned.1.call-done, f32[512,2816]{1,0:T(8,128)} %fusion.115), kind=kOutput, calls=%fused_computation.108 | convolution fusion | flops 8128823296 | bytes 24510464 | tf_op jit(solution)/shard_map/dot_general | solution.py:47
  395.1 2.5 copy.74
  397.6 1.6 copy.72
  399.3 36.0 %reduce-scatter.5.cloned.1.call-done = bf16[512,704]{0,1:T(8,128)(2,1)} async-done(((bf16[512,2816]{0,1:T(8,128)(2,1)}), bf16[512,704]{0,1:T(8,128)(2,1)}) %reduce-scatter.5.cloned.1.call-update) | async-done | bytes 720912 | tf_op jit(solution)/shard_map/reduce_scatter | solution.py:48
  435.3 3.5 fusion.109
  438.8 0.6 reduce-scatter.7.cloned.1.call-start
  439.4 41.4 %all-gather.11.cloned.1.call-done = bf16[512,2816]{0,1:T(8,128)(2,1)} async-done(((bf16[512,704]{0,1:T(8,128)(2,1)}), bf16[512,2816]{0,1:T(8,128)(2,1)}) %all-gather.11.cloned.1.call-update) | async-done | bytes 2883600 | tf_op jit(solution)/shard_map/all_gather | solution.py:56
  480.7 16.0 %fusion.5 = bf16[512,2816]{1,0:T(8,128)(2,1)S(1)} fusion(f32[512,2816]{1,0:T(8,128)} %fusion.115, bf16[512,2816]{0,1:T(8,128)(2,1)} %all-gather.11.cloned.1.call-done, bf16[2816,2816]{0,1:T(8,128)(2,1)} %all-gather.9.cloned.1.call-done), kind=kOutput, calls=%fused_computation.104 | convolution fusion | flops 8134590464 | bytes 27394048 | tf_op jit(solution)/shard_map/dot_general | solution.py:57
  496.8 1.6 copy-done.7
  498.3 13.0 %convolution_convert_fusion.2 = bf16[512,2816]{0,1:T(8,128)(2,1)} fusion(bf16[512,2816]{1,0:T(8,128)(2,1)S(1)} %fusion.5, bf16[2816,2816]{1,0:T(8,128)(2,1)} %all-gather.7.cloned.1.call-done), kind=kOutput, calls=%fused_computation.107 | convolution fusion | flops 8121614336 | bytes 21626880 | tf_op jit(solution)/shard_map/dot_general | solution.py:71
  511.4 41.9 %reduce-scatter.7.cloned.1.call-done = bf16[512,704]{0,1:T(8,128)(2,1)} async-done(((bf16[512,2816]{0,1:T(8,128)(2,1)}), bf16[512,704]{0,1:T(8,128)(2,1)}) %reduce-scatter.7.cloned.1.call-update) | async-done | bytes 720912 | tf_op jit(solution)/shard_map/reduce_scatter | solution.py:74
  553.3 1.7 fusion.113
  555.0 9.1 all-reduce.2
  564.1 2.6 fusion.111
  566.8 1.8 copy.75
  568.6 3.8 multiply_reduce_fusion.2
  572.4 4.2 multiply_reduce_fusion
  576.7 4.5 multiply_reduce_fusion.1
  582.2 0.6 copy-done.3
  582.9 15.4 %convolution_convert_fusion = bf16[2816,2816]{1,0:T(8,128)(2,1)} fusion(bf16[512,2816]{0,1:T(8,128)(2,1)} %all-gather.11.cloned.1.call-done, f32[512,2816]{1,0:T(8,128)} %fusion.115), kind=kOutput, calls=%fused_computation.96 | convolution fusion | flops 8135311360 | bytes 24510464 | tf_op jit(solution)/shard_map/dot_general | solution.py:80
  598.6 13.9 %convolution_convert_fusion.1 = bf16[2816,2816]{1,0:T(8,128)(2,1)} fusion(bf16[512,2816]{0,1:T(8,128)(2,1)} %all-gather.5.cloned.1.call-done, bf16[512,2816]{1,0:T(8,128)(2,1)} %copy-done.7), kind=kOutput, calls=%fused_computation.97 | convolution fusion | flops 8128102400 | bytes 21626880 | tf_op jit(solution)/shard_map/dot_general | solution.py:64
  612.6 2.4 copy.73
  615.2 14.6 %all-reduce.3 = (bf16[704]{0:T(1024)(128)(2,1)S(1)}, bf16[704]{0:T(1024)(128)(2,1)S(1)}, bf16[704]{0:T(1024)(128)(2,1)S(1)}) all-reduce(bf16[704]{0:T(1024)(128)(2,1)S(1)} %get-tuple-element.64, bf16[704]{0:T(1024)(128)(2,1)S(1)} %reduce_sum.567, bf16[704]{0:T(1024)(128)(2,1)S(1)} %get-tuple-element.124), channel_id=1, replica_groups=mesh['dp'=8,'chan'=4] {'dp'}, use_global_device_ids=true, to_apply=%region_61.62 | all-reduce | flops 2112 | bytes 8448 | tf_op jit(solution)/shard_map/psum | solution.py:124
  629.8 0.6 convert_element_type.85
  630.4 0.6 convert_element_type.86
  631.0 0.6 convert_element_type.91
  631.6 12.3 %fusion.102 = bf16[2,16,16,704]{3,2,1,0:T(8,128)(2,1)} fusion(f32[2,16,16,704]{3,2,1,0:T(8,128)S(1)} %bitcast.82, f32[704]{0:T(1024)S(1)} %get-tuple-element.115, f32[704]{0:T(1024)S(1)} %get-tuple-element.116, f32[704]{0:T(1024)S(1)} %get-tuple-element.69, f32[704]{0:T(1024)S(1)} %get-tuple-element.70, f32[704]{0:T(1024)S(1)} %get-tuple-element.71, ...), kind=kLoop, calls=%fused_computation.210 | loop fusion | flops 36044800 | bytes 3021568 | tf_op jit(solution)/shard_map/convert_element_type | solution.py:121
  643.9 1.6 convert_element_type.83
  645.5 152.7 %reduce-scatter.11.cloned.1.call-done = bf16[352,2816]{1,0:T(8,128)(2,1)} async-done(((bf16[2816,2816]{1,0:T(8,128)(2,1)}), bf16[352,2816]{1,0:T(8,128)(2,1)}) %reduce-scatter.11.cloned.1.call-update) | async-done | bytes 1982480 | tf_op jit(solution)/shard_map/reduce_scatter | solution.py:79
  798.2 3.7 convert_bitcast_fusion
  801.9 156.8 %reduce-scatter.9.cloned.1.call-done = bf16[352,2816]{1,0:T(8,128)(2,1)} async-done(((bf16[2816,2816]{1,0:T(8,128)(2,1)}), bf16[352,2816]{1,0:T(8,128)(2,1)}) %reduce-scatter.9.cloned.1.call-update) | async-done | bytes 1982480 | tf_op jit(solution)/shard_map/reduce_scatter | solution.py:63
  958.7 3.7 convert_element_type.88
  (100 shorter events, 2.0 us)
Async XLA Ops:
  7.2 82.8 %all-gather.5.cloned.1.call-start = ((), (), s32[]{:S(2)}) async-start(), calls=%async_computation.4 | async-start | bytes 3604480 | tf_op jit(solution)/shard_map/all_gather | solution.py:42
  24.8 19.9 %copy-start = (f32[2,16,16,704]{3,2,1,0:T(8,128)}, f32[2,16,16,704]{3,2,1,0:T(8,128)S(1)}, u32[]{:S(2)}) copy-start(f32[2,16,16,704]{3,2,1,0:T(8,128)S(1)} %get-tuple-element.123) | copy-start | bytes 4325380
  36.6 9.9 %copy-start.4 = (f32[704]{0:T(1024)S(1)}, f32[704]{0:T(1024)}, u32[]{:S(2)}) copy-start(f32[704]{0:T(1024)} %param.10) | copy-start | bytes 8452
  36.6 9.9 %copy-start.5 = (f32[704]{0:T(1024)S(1)}, f32[704]{0:T(1024)}, u32[]{:S(2)}) copy-start(f32[704]{0:T(1024)} %param.11) | copy-start | bytes 8452
  47.7 187.5 %all-gather.7.cloned.1.call-start = ((), (), s32[]{:S(2)}) async-start(), calls=%async_computation.5 | async-start | bytes 17842176 | tf_op jit(solution)/shard_map/all_gather | solution.py:43
  48.5 330.3 %all-gather.9.cloned.1.call-start = ((), (), s32[]{:S(2)}) async-start(), calls=%async_computation.6 | async-start | bytes 17842176 | tf_op jit(solution)/shard_map/all_gather | solution.py:46
  49.2 386.0 %reduce-scatter.5.cloned.1.call-start = ((), (), s32[]{:S(2)}) async-start(), calls=%async_computation.7 | async-start | bytes 3604480 | tf_op jit(solution)/shard_map/reduce_scatter | solution.py:48
  395.1 85.6 %all-gather.11.cloned.1.call-start = ((), (), s32[]{:S(2)}) async-start(), calls=%async_computation.8 | async-start | bytes 3604480 | tf_op jit(solution)/shard_map/all_gather | solution.py:56
  397.6 37.6 %copy-start.6 = (f32[704]{0:T(1024)S(1)}, f32[704]{0:T(1024)}, u32[]{:S(2)}) copy-start(f32[704]{0:T(1024)} %param.14) | copy-start | bytes 8452
  438.8 114.5 %reduce-scatter.7.cloned.1.call-start = ((), (), s32[]{:S(2)}) async-start(), calls=%async_computation.9 | async-start | bytes 3604480 | tf_op jit(solution)/shard_map/reduce_scatter | solution.py:74
  496.8 1.6 copy-start.7
  511.4 132.5 %all-reduce.6.cloned.1.call-start = ((), (), s32[]{:S(2)}) async-start(), calls=%async_computation.10 | async-start | bytes 172032 | tf_op jit(solution)/shard_map/psum | solution.py:123
  582.2 0.6 copy-start.3
  582.9 215.3 %reduce-scatter.11.cloned.1.call-start = ((), (), s32[]{:S(2)}) async-start(), calls=%async_computation.12 | async-start | bytes 17842176 | tf_op jit(solution)/shard_map/reduce_scatter | solution.py:79
  598.4 360.3 %reduce-scatter.9.cloned.1.call-start = ((), (), s32[]{:S(2)}) async-start(), calls=%async_computation.11 | async-start | bytes 17842176 | tf_op jit(solution)/shard_map/reduce_scatter | solution.py:63
  612.6 2.4 copy-start.1
  612.6 19.0 %copy-start.2 = (bf16[2,16,16,704]{3,2,1,0:T(8,128)(2,1)S(1)}, bf16[2,16,16,704]{3,2,1,0:T(8,128)(2,1)}, u32[]{:S(2)}) copy-start(bf16[2,16,16,704]{3,2,1,0:T(8,128)(2,1)} %param.15) | copy-start | bytes 2162692
Sparse Core Ops, SparseCore 0:
  47.9 42.1 all-gather.4
  91.7 143.5 all-gather.6
  236.9 141.8 all-gather.8
  395.2 39.9 reduce-scatter.4
  438.9 41.7 all-gather.10
  511.5 41.7 reduce-scatter.6
  583.0 49.9 all-reduce.5
  635.5 162.6 reduce-scatter.10
  800.7 157.9 reduce-scatter.8
where the time goes:
time: 974 us; the launch traced here: 969 us
  waiting for transfers between devices  744 us (76%)
  matrix products  89.7 us (9%)
  other arithmetic  58.8 us (6%)
  blocking collectives  43 us (4%)
  local copies, waits for them, and re-layouts  17.3 us (2%)
  between operations  14.7 us (2%)
    reduce_scatter x1, waiting for transfers between devices, body(): lax.psum_scatter(lax.dot_general(columns, dpre, (((0,), (0,)), ((), ())),...  157 us
    reduce_scatter x1, waiting for transfers between devices, body(): lax.psum_scatter(lax.dot_general(columns, hidden, (((0,), (0,)), ((), ())...  153 us
    all_gather x1, waiting for transfers between devices, body(): expand_all = lax.all_gather(w_expand, 'dp', axis=0, tiled=True)  145 us
    all_gather x1, waiting for transfers between devices, body(): reduce_all = lax.all_gather(w_reduce, 'dp', axis=1, tiled=True)  128 us
    reduce_scatter x1, waiting for transfers between devices, body(): lax.psum_scatter(partial_normed.astype(jnp.bfloat16), 'chan', scatter_dim...  41.9 us
    all_gather x1, waiting for transfers between devices, body(): dbranch_all = lax.all_gather(dbranch, 'chan', axis=1, tiled=True)  41.4 us
    all_gather x1, waiting for transfers between devices, body(): normed_all = lax.all_gather(normed_output, 'chan', axis=1, tiled=True)  40.4 us
    reduce_scatter x1, waiting for transfers between devices, body(): lax.psum_scatter(partial_branch.astype(jnp.bfloat16), 'chan', scatter_dim...  36 us
  transfers between devices with their start and end apart: 9, of which 8 were waited for; matrix products, arithmetic and copies ran while one was open for 7% of the time, Pallas kernels for 0%

commit v1 on v0

--- a/solution.py
+++ b/solution.py
@@ -5,6 +5,19 @@
 from jax.sharding import PartitionSpec as P
 
 eps = 1e-06
+
+
+def gather_around(x, axis, dim):
+    length, index, rows = (lax.axis_size(axis), lax.axis_index(axis), x.shape[dim])
+    upward = [(i, (i + 1) % length) for i in range(length)]
+    whole = jnp.zeros((*x.shape[:dim], length * rows, *x.shape[dim + 1 :]), x.dtype)
+    block = x
+    for step in range(length):
+        owner = (index - step) % length
+        whole = lax.dynamic_update_slice_in_dim(whole, block, owner * rows, axis=dim)
+        if step < length - 1:
+            block = lax.ppermute(block, axis, upward)
+    return whole
 
 
 def depthwise(field, kern):
@@ -39,7 +52,7 @@
     inverse_deviation = lax.rsqrt(var + eps)
     standardized_input = centred_rows * inverse_deviation
     normed_output = (standardized_input * layernorm_gain + layernorm_bias).astype(jnp.bfloat16)
-    normed_all = lax.all_gather(normed_output, "chan", axis=1, tiled=True)
+    normed_all = gather_around(normed_output, "chan", 1)
     expand_all = lax.all_gather(w_expand, "dp", axis=0, tiled=True)
     pre = jnp.dot(normed_all, expand_all, preferred_element_type=jnp.float32)
     hidden = (pre * normal_cdf(pre)).astype(jnp.bfloat16)

time: 974 us -> 895 us (0.919)
  waiting for transfers between devices: 744 us -> 658 us
    all_gather x1, waiting for transfers between devices: 145 us -> 58.6 us  [body(): expand_all = lax.all_gather(w_expand, 'dp', axis=0, tiled=True)]
    ppermute x0 -> x3, waiting for transfers between devices: none -> 40.9 us  [gather_around(): block = lax.ppermute(block, axis, upward)]
    all_gather x1 -> x0, waiting for transfers between devices: 40.4 us -> none  [body(): normed_all = lax.all_gather(normed_output, 'chan', axis=1, tiled=True)]
  transfers between devices with their start and end apart: 9 -> 11, of which waited for: 8 -> 10; matrix products, arithmetic and copies ran while one was open for 7% -> 11% of each run, Pallas kernels for 0% -> 0%
where the time goes in v1:
time: 895 us; the launch traced here: 890 us
  waiting for transfers between devices  658 us (74%)
  matrix products  89.7 us (10%)
  other arithmetic  57.7 us (6%)
  blocking collectives  43 us (5%)
  local copies, waits for them, and re-layouts  23.1 us (3%)
  between operations  15.1 us (2%)
    reduce_scatter x1, waiting for transfers between devices, body(): lax.psum_scatter(lax.dot_general(columns, dpre, (((0,), (0,)), ((), ())),...  157 us
    reduce_scatter x1, waiting for transfers between devices, body(): lax.psum_scatter(lax.dot_general(columns, hidden, (((0,), (0,)), ((), ())...  153 us
    all_gather x1, waiting for transfers between devices, body(): reduce_all = lax.all_gather(w_reduce, 'dp', axis=1, tiled=True)  128 us
    all_gather x1, waiting for transfers between devices, body(): expand_all = lax.all_gather(w_expand, 'dp', axis=0, tiled=True)  58.6 us
    reduce_scatter x1, waiting for transfers between devices, body(): lax.psum_scatter(partial_normed.astype(jnp.bfloat16), 'chan', scatter_dim...  41.9 us
    all_gather x1, waiting for transfers between devices, body(): dbranch_all = lax.all_gather(dbranch, 'chan', axis=1, tiled=True)  41.4 us
    ppermute x3, waiting for transfers between devices, gather_around(): block = lax.ppermute(block, axis, upward)  40.9 us
    reduce_scatter x1, waiting for transfers between devices, body(): lax.psum_scatter(partial_branch.astype(jnp.bfloat16), 'chan', scatter_dim...  36 us
  transfers between devices with their start and end apart: 11, of which 10 were waited for; matrix products, arithmetic and copies ran while one was open for 11% of the time, Pallas kernels for 0%

profile of v1, /device:TPU:0, one launch (start us, length us, event | category | flops | bytes accessed | tf_op | source)
XLA Modules:
  0.0 890.3 jit_solution(8187435653636099195)
XLA Ops:
  7.2 0.7 all-gather.4.cloned.1.call-update
  8.0 0.7 all-gather.6.cloned.1.call-update
  8.9 0.7 copy-done.5
  10.0 12.3 %fusion.114 = (f32[2,16,16]{2,1,0:T(8,128)S(1)}, f32[2,16,16,704]{3,2,1,0:T(8,128)S(1)}) fusion(f32[704]{0:T(1024)S(1)} %get-tuple-element.115, f32[704]{0:T(1024)S(1)} %get-tuple-element.116, f32[704]{0:T(1024)S(1)} %get-tuple-element.69, f32[704]{0:T(1024)S(1)} %get-tuple-element.70, f32[704]{0:T(1024)S(1)} %get-tuple-element.71, ...), kind=kLoop, calls=%fused_computation.340 | loop fusion | flops 35323392 | bytes 3023616 | tf_op jit(solution)/shard_map/reduce_sum | solution.py:49
  22.4 11.3 %psum.56 = f32[512]{0:T(512)S(1)} all-reduce(f32[512]{0:T(512)S(1)} %reduce_sum.512), channel_id=1, replica_groups=mesh['dp'=8,'chan'=4] {'chan'}, use_global_device_ids=true, to_apply=%region_1.2 | all-reduce | flops 512 | bytes 4096 | tf_op jit(solution)/shard_map/psum | solution.py:49
  34.2 1.9 copy.71
  36.1 8.0 psum.57
  44.1 1.8 broadcast_in_dim.2
  45.9 1.1 constant_dynamic-update-slice_fusion.10
  47.1 1.5 collective-permute-start
  48.5 14.9 %collective-permute-done = bf16[512,704]{0,1:T(8,128)(2,1)S(1)} collective-permute-done((bf16[512,704]{0,1:T(8,128)(2,1)S(1)}, bf16[512,704]{0,1:T(8,128)(2,1)S(1)}, u32[]{:S(2)}, u32[]{:S(2)}) %collective-permute-start) | collective-permute-done | bytes 720928 | tf_op jit(solution)/shard_map/ppermute | solution.py:19
  63.4 0.9 copy-done.4
  64.8 15.3 %collective-permute-done.1 = bf16[512,704]{0,1:T(8,128)(2,1)} collective-permute-done((bf16[512,704]{0,1:T(8,128)(2,1)S(1)}, bf16[512,704]{0,1:T(8,128)(2,1)}, u32[]{:S(2)}, u32[]{:S(2)}) %collective-permute-start.1) | collective-permute-done | bytes 720928 | tf_op jit(solution)/shard_map/ppermute | solution.py:19
  80.4 2.1 constant_dynamic-update-slice_fusion.9
  82.5 2.0 constant_dynamic-update-slice_fusion.8
  84.5 10.8 %collective-permute-done.2 = bf16[512,704]{0,1:T(8,128)(2,1)} collective-permute-done((bf16[512,704]{0,1:T(8,128)(2,1)}, bf16[512,704]{0,1:T(8,128)(2,1)}, u32[]{:S(2)}, u32[]{:S(2)}) %collective-permute-start.2) | collective-permute-done | bytes 720928 | tf_op jit(solution)/shard_map/ppermute | solution.py:19
  95.3 2.0 constant_dynamic-update-slice_fusion.7
  97.3 58.6 %all-gather.4.cloned.1.call-done = bf16[2816,2816]{1,0:T(8,128)(2,1)} async-done(((bf16[352,2816]{1,0:T(8,128)(2,1)}), bf16[2816,2816]{1,0:T(8,128)(2,1)}) %all-gather.4.cloned.1.call-update) | async-done | bytes 15859728 | tf_op jit(solution)/shard_map/all_gather | solution.py:56
  156.0 15.1 %fusion.115 = f32[512,2816]{1,0:T(8,128)} fusion(bf16[512,2816]{0,1:T(8,128)(2,1)} %constant_dynamic-update-slice_fusion.7, bf16[2816,2816]{1,0:T(8,128)(2,1)} %all-gather.4.cloned.1.call-done), kind=kOutput, calls=%fused_computation.341 | convolution fusion | flops 8120172544 | bytes 24510464 | tf_op jit(solution)/shard_map/dot_general | solution.py:57
  171.1 128.5 %all-gather.6.cloned.1.call-done = bf16[2816,2816]{0,1:T(8,128)(2,1)} async-done(((bf16[2816,352]{0,1:T(8,128)(2,1)}), bf16[2816,2816]{0,1:T(8,128)(2,1)}) %all-gather.6.cloned.1.call-update) | async-done | bytes 15859728 | tf_op jit(solution)/shard_map/all_gather | solution.py:59
  299.5 16.3 %convolution_convert_fusion.3 = bf16[512,2816]{0,1:T(8,128)(2,1)} fusion(bf16[2816,2816]{0,1:T(8,128)(2,1)} %all-gather.6.cloned.1.call-done, f32[512,2816]{1,0:T(8,128)} %fusion.115), kind=kOutput, calls=%fused_computation.108 | convolution fusion | flops 8128823296 | bytes 24510464 | tf_op jit(solution)/shard_map/dot_general | solution.py:60
  315.8 2.5 copy.74
  318.3 1.6 copy.72
  319.9 36.0 %reduce-scatter.5.cloned.1.call-done = bf16[512,704]{0,1:T(8,128)(2,1)} async-done(((bf16[512,2816]{0,1:T(8,128)(2,1)}), bf16[512,704]{0,1:T(8,128)(2,1)}) %reduce-scatter.5.cloned.1.call-update) | async-done | bytes 720912 | tf_op jit(solution)/shard_map/reduce_scatter | solution.py:61
  355.9 3.5 fusion.109
  360.1 41.4 %all-gather.8.cloned.1.call-done = bf16[512,2816]{0,1:T(8,128)(2,1)} async-done(((bf16[512,704]{0,1:T(8,128)(2,1)}), bf16[512,2816]{0,1:T(8,128)(2,1)}) %all-gather.8.cloned.1.call-update) | async-done | bytes 2883600 | tf_op jit(solution)/shard_map/all_gather | solution.py:69
  401.4 16.0 %fusion.5 = bf16[512,2816]{1,0:T(8,128)(2,1)S(1)} fusion(f32[512,2816]{1,0:T(8,128)} %fusion.115, bf16[512,2816]{0,1:T(8,128)(2,1)} %all-gather.8.cloned.1.call-done, bf16[2816,2816]{0,1:T(8,128)(2,1)} %all-gather.6.cloned.1.call-done), kind=kOutput, calls=%fused_computation.104 | convolution fusion | flops 8134590464 | bytes 27394048 | tf_op jit(solution)/shard_map/dot_general | solution.py:70
  417.5 1.6 copy-done.10
  419.1 13.0 %convolution_convert_fusion.2 = bf16[512,2816]{0,1:T(8,128)(2,1)} fusion(bf16[512,2816]{1,0:T(8,128)(2,1)S(1)} %fusion.5, bf16[2816,2816]{1,0:T(8,128)(2,1)} %all-gather.4.cloned.1.call-done), kind=kOutput, calls=%fused_computation.107 | convolution fusion | flops 8121614336 | bytes 21626880 | tf_op jit(solution)/shard_map/dot_general | solution.py:84
  432.2 41.9 %reduce-scatter.7.cloned.1.call-done = bf16[512,704]{0,1:T(8,128)(2,1)} async-done(((bf16[512,2816]{0,1:T(8,128)(2,1)}), bf16[512,704]{0,1:T(8,128)(2,1)}) %reduce-scatter.7.cloned.1.call-update) | async-done | bytes 720912 | tf_op jit(solution)/shard_map/reduce_scatter | solution.py:87
  474.1 1.7 fusion.113
  475.8 9.1 %all-reduce.2 = (f32[512]{0:T(512)S(1)}, f32[512]{0:T(512)S(1)}) all-reduce(f32[512]{0:T(512)S(1)} %get-tuple-element.65, f32[512]{0:T(512)S(1)} %get-tuple-element.67), channel_id=1, replica_groups=mesh['dp'=8,'chan'=4] {'chan'}, use_global_device_ids=true, to_apply=%region_9.10 | all-reduce | flops 1024 | bytes 8192 | tf_op jit(solution)/shard_map/psum | solution.py:106
  484.9 2.6 fusion.111
  487.5 1.8 copy.75
  489.4 3.8 multiply_reduce_fusion.2
  493.2 4.2 multiply_reduce_fusion
  497.4 4.5 multiply_reduce_fusion.1
  503.0 0.6 copy-done.6
  503.7 15.4 %convolution_convert_fusion = bf16[2816,2816]{1,0:T(8,128)(2,1)} fusion(bf16[512,2816]{0,1:T(8,128)(2,1)} %all-gather.8.cloned.1.call-done, f32[512,2816]{1,0:T(8,128)} %fusion.115), kind=kOutput, calls=%fused_computation.96 | convolution fusion | flops 8135311360 | bytes 24510464 | tf_op jit(solution)/shard_map/dot_general | solution.py:93
  519.4 13.9 %convolution_convert_fusion.1 = bf16[2816,2816]{1,0:T(8,128)(2,1)} fusion(bf16[512,2816]{0,1:T(8,128)(2,1)} %constant_dynamic-update-slice_fusion.7, bf16[512,2816]{1,0:T(8,128)(2,1)} %copy-done.10), kind=kOutput, calls=%fused_computation.97 | convolution fusion | flops 8128102400 | bytes 21626880 | tf_op jit(solution)/shard_map/dot_general | solution.py:77
  533.3 2.4 copy.73
  535.9 14.6 %all-reduce.3 = (bf16[704]{0:T(1024)(128)(2,1)S(1)}, bf16[704]{0:T(1024)(128)(2,1)S(1)}, bf16[704]{0:T(1024)(128)(2,1)S(1)}) all-reduce(bf16[704]{0:T(1024)(128)(2,1)S(1)} %get-tuple-element.64, bf16[704]{0:T(1024)(128)(2,1)S(1)} %reduce_sum.567, bf16[704]{0:T(1024)(128)(2,1)S(1)} %get-tuple-element.126), channel_id=1, replica_groups=mesh['dp'=8,'chan'=4] {'dp'}, use_global_device_ids=true, to_apply=%region_61.62 | all-reduce | flops 2112 | bytes 8448 | tf_op jit(solution)/shard_map/psum | solution.py:137
  552.3 12.3 %fusion.102 = bf16[2,16,16,704]{3,2,1,0:T(8,128)(2,1)} fusion(f32[2,16,16,704]{3,2,1,0:T(8,128)S(1)} %bitcast.82, f32[704]{0:T(1024)S(1)} %get-tuple-element.115, f32[704]{0:T(1024)S(1)} %get-tuple-element.116, f32[704]{0:T(1024)S(1)} %get-tuple-element.69, f32[704]{0:T(1024)S(1)} %get-tuple-element.70, f32[704]{0:T(1024)S(1)} %get-tuple-element.71, ...), kind=kLoop, calls=%fused_computation.210 | loop fusion | flops 36044800 | bytes 3021568 | tf_op jit(solution)/shard_map/convert_element_type | solution.py:134
  564.6 1.6 convert_element_type.83
  566.2 152.7 %reduce-scatter.11.cloned.1.call-done = bf16[352,2816]{1,0:T(8,128)(2,1)} async-done(((bf16[2816,2816]{1,0:T(8,128)(2,1)}), bf16[352,2816]{1,0:T(8,128)(2,1)}) %reduce-scatter.11.cloned.1.call-update) | async-done | bytes 1982480 | tf_op jit(solution)/shard_map/reduce_scatter | solution.py:92
  719.0 3.7 convert_bitcast_fusion
  722.7 156.7 %reduce-scatter.9.cloned.1.call-done = bf16[352,2816]{1,0:T(8,128)(2,1)} async-done(((bf16[2816,2816]{1,0:T(8,128)(2,1)}), bf16[352,2816]{1,0:T(8,128)(2,1)}) %reduce-scatter.9.cloned.1.call-update) | async-done | bytes 1982480 | tf_op jit(solution)/shard_map/reduce_scatter | solution.py:76
  879.5 3.7 convert_element_type.88
  (113 shorter events, 5.8 us)
Async XLA Ops:
  7.2 1.6 copy-start.2
  7.2 148.8 %all-gather.4.cloned.1.call-start = ((), (), s32[]{:S(2)}) async-start(), calls=%async_computation.4 | async-start | bytes 17842176 | tf_op jit(solution)/shard_map/all_gather | solution.py:56
  7.9 291.6 %all-gather.6.cloned.1.call-start = ((), (), s32[]{:S(2)}) async-start(), calls=%async_computation.5 | async-start | bytes 17842176 | tf_op jit(solution)/shard_map/all_gather | solution.py:59
  8.7 0.9 copy-start.5
  8.7 347.3 %reduce-scatter.5.cloned.1.call-start = ((), (), s32[]{:S(2)}) async-start(), calls=%async_computation.6 | async-start | bytes 3604480 | tf_op jit(solution)/shard_map/reduce_scatter | solution.py:61
  22.3 11.9 %copy-start = (f32[2,16,16,704]{3,2,1,0:T(8,128)}, f32[2,16,16,704]{3,2,1,0:T(8,128)S(1)}, u32[]{:S(2)}) copy-start(f32[2,16,16,704]{3,2,1,0:T(8,128)S(1)} %get-tuple-element.125) | copy-start | bytes 4325380
  36.1 9.8 %copy-start.7 = (f32[704]{0:T(1024)S(1)}, f32[704]{0:T(1024)}, u32[]{:S(2)}) copy-start(f32[704]{0:T(1024)} %param.10) | copy-start | bytes 8452
  36.1 9.8 %copy-start.8 = (f32[704]{0:T(1024)S(1)}, f32[704]{0:T(1024)}, u32[]{:S(2)}) copy-start(f32[704]{0:T(1024)} %param.11) | copy-start | bytes 8452
  47.1 16.3 %collective-permute-start = (bf16[512,704]{0,1:T(8,128)(2,1)S(1)}, bf16[512,704]{0,1:T(8,128)(2,1)S(1)}, u32[]{:S(2)}, u32[]{:S(2)}) collective-permute-start(bf16[512,704]{0,1:T(8,128)(2,1)S(1)} %get-tuple-element.123), channel_id=1, source_target_pairs={{0,1},{1,2},{2,3},{3,0},{4,5},{5,6},{6,7},{7,4},{8,9},{9,10},{10,1... | collective-permute-start | bytes 2162696 | tf_op jit(solution)/shard_map/ppermute | solution.py:19
  63.4 0.9 copy-start.4
  64.2 15.8 %collective-permute-start.1 = (bf16[512,704]{0,1:T(8,128)(2,1)S(1)}, bf16[512,704]{0,1:T(8,128)(2,1)}, u32[]{:S(2)}, u32[]{:S(2)}) collective-permute-start(bf16[512,704]{0,1:T(8,128)(2,1)S(1)} %collective-permute-done), channel_id=1, source_target_pairs={{0,1},{1,2},{2,3},{3,0},{4,5},{5,6},{6,7},{7,4},{8,9},{9,10},{10,1... | collective-permute-start | bytes 2162696 | tf_op jit(solution)/shard_map/ppermute | solution.py:19
  80.1 15.3 %collective-permute-start.2 = (bf16[512,704]{0,1:T(8,128)(2,1)}, bf16[512,704]{0,1:T(8,128)(2,1)}, u32[]{:S(2)}, u32[]{:S(2)}) collective-permute-start(bf16[512,704]{0,1:T(8,128)(2,1)} %collective-permute-done.1), channel_id=1, source_target_pairs={{0,1},{1,2},{2,3},{3,0},{4,5},{5,6},{6,7},{7,4},{8,9},{9,10},{10,1... | collective-permute-start | bytes 2162696 | tf_op jit(solution)/shard_map/ppermute | solution.py:19
  315.8 85.6 %all-gather.8.cloned.1.call-start = ((), (), s32[]{:S(2)}) async-start(), calls=%async_computation.7 | async-start | bytes 3604480 | tf_op jit(solution)/shard_map/all_gather | solution.py:69
  318.3 37.6 %copy-start.9 = (f32[704]{0:T(1024)S(1)}, f32[704]{0:T(1024)}, u32[]{:S(2)}) copy-start(f32[704]{0:T(1024)} %param.14) | copy-start | bytes 8452
  359.5 114.6 %reduce-scatter.7.cloned.1.call-start = ((), (), s32[]{:S(2)}) async-start(), calls=%async_computation.8 | async-start | bytes 3604480 | tf_op jit(solution)/shard_map/reduce_scatter | solution.py:87
  417.5 1.6 copy-start.10
  432.2 132.5 %all-reduce.6.cloned.1.call-start = ((), (), s32[]{:S(2)}) async-start(), calls=%async_computation.9 | async-start | bytes 172032 | tf_op jit(solution)/shard_map/psum | solution.py:136
  503.0 0.6 copy-start.6
  503.6 215.3 %reduce-scatter.11.cloned.1.call-start = ((), (), s32[]{:S(2)}) async-start(), calls=%async_computation.11 | async-start | bytes 17842176 | tf_op jit(solution)/shard_map/reduce_scatter | solution.py:92
  519.1 360.3 %reduce-scatter.9.cloned.1.call-start = ((), (), s32[]{:S(2)}) async-start(), calls=%async_computation.10 | async-start | bytes 17842176 | tf_op jit(solution)/shard_map/reduce_scatter | solution.py:76
  533.3 2.4 copy-start.1
  533.3 19.0 %copy-start.3 = (bf16[2,16,16,704]{3,2,1,0:T(8,128)(2,1)S(1)}, bf16[2,16,16,704]{3,2,1,0:T(8,128)(2,1)}, u32[]{:S(2)}) copy-start(bf16[2,16,16,704]{3,2,1,0:T(8,128)(2,1)} %param.15) | copy-start | bytes 2162692
Sparse Core Ops, SparseCore 0:
  9.7 146.2 all-gather.3
  157.6 141.8 all-gather.5
  315.9 39.9 reduce-scatter.4
  359.6 41.7 all-gather.7
  432.3 41.7 reduce-scatter.6
  503.8 49.9 all-reduce.5
  556.3 162.6 reduce-scatter.10
  721.4 157.9 reduce-scatter.8
